TPU v7x, 32 devices: a whole 2x2x4 slice. The times are simulated.
32 devices in a mesh: dp: 16 (over z, y, x), tensor: 2 (over core).
Axes of the slice: x: 2, y: 2, z: 4, core: 2. Of those that a mesh axis runs over, the one named last changes fastest.
Arguments:
- tokens: bfloat16 [16384, 768], P('dp'), may hold values from -6 to 6
- cotangent: bfloat16 [16384, 768], P('dp'), may hold values from -6 to 6
- lengths: int32 [32], P('dp'), may hold values from 113 to 512, as said below
- proj_weight: float32 [2, 768, 3, 768], P(None, 'dp', None, 'tensor'), may hold values from -0.21875 to 0.21875
- out_weight: float32 [2, 768, 768], P(None, 'dp', 'tensor'), may hold values from -0.875 to 0.875
- up_weight: float32 [2, 768, 3072], P(None, 'dp', 'tensor'), may hold values from -0.21875 to 0.21875
- down_weight: float32 [2, 768, 3072], P(None, 'dp', 'tensor'), may hold values from -0.109375 to 0.109375
- small_params: float32 [2, 8448], replicated, may hold values from -0.8 to 1.4
- proj_first: float32 [2, 768, 3, 768], P(None, 'dp', None, 'tensor'), may hold values from -0.00018310547 to 0.00018310547
- proj_second: float32 [2, 768, 3, 768], P(None, 'dp', None, 'tensor'), may hold values from 3.527916e-11 to 3.52791626e-09
- out_first: float32 [2, 768, 768], P(None, 'dp', 'tensor'), may hold values from -0.00018310547 to 0.00018310547
- out_second: float32 [2, 768, 768], P(None, 'dp', 'tensor'), may hold values from 7.0558325e-12 to 7.0558325e-10
- up_first: float32 [2, 768, 3072], P(None, 'dp', 'tensor'), may hold values from -0.00018310547 to 0.00018310547
- up_second: float32 [2, 768, 3072], P(None, 'dp', 'tensor'), may hold values from 3.527916e-11 to 3.52791626e-09
- down_first: float32 [2, 768, 3072], P(None, 'dp', 'tensor'), may hold values from -0.00018310547 to 0.00018310547
- down_second: float32 [2, 768, 3072], P(None, 'dp', 'tensor'), may hold values from 3.527916e-11 to 3.52791626e-09
- small_first: float32 [2, 8448], replicated, may hold values from -0.00018310547 to 0.00018310547
- small_second: float32 [2, 8448], replicated, may hold values from 3.527916e-11 to 5.644666e-10
Outputs:
- activations: float32 [16384, 768], P('dp')
- input_grad: float32 [16384, 768], P('dp')
- grad_norm: float32 [], replicated
- proj_first_new: float32 [2, 768, 3, 768], P(None, 'dp', None, 'tensor')
- proj_second_new: float32 [2, 768, 3, 768], P(None, 'dp', None, 'tensor')
- proj_weight_new: float32 [2, 768, 3, 768], P(None, 'dp', None, 'tensor')
- out_first_new: float32 [2, 768, 768], P(None, 'dp', 'tensor')
- out_second_new: float32 [2, 768, 768], P(None, 'dp', 'tensor')
- out_weight_new: float32 [2, 768, 768], P(None, 'dp', 'tensor')
- up_first_new: float32 [2, 768, 3072], P(None, 'dp', 'tensor')
- up_second_new: float32 [2, 768, 3072], P(None, 'dp', 'tensor')
- up_weight_new: float32 [2, 768, 3072], P(None, 'dp', 'tensor')
- down_first_new: float32 [2, 768, 3072], P(None, 'dp', 'tensor')
- down_second_new: float32 [2, 768, 3072], P(None, 'dp', 'tensor')
- down_weight_new: float32 [2, 768, 3072], P(None, 'dp', 'tensor')
- small_first_new: float32 [2, 8448], replicated
- small_second_new: float32 [2, 8448], replicated
- small_params_new: float32 [2, 8448], replicated
Inputs may be any that keep to these rules, and one draw needn't show every extreme that they name: `lengths`: each length is 512, 256 or 128, reduced by less than max(1, 16); the first sequence has length 512.
All inputs are finite; a program needn't handle non-finite values.
Results may differ from a plain program's by a relative error of at most 0.03.
The roundings to bfloat16 on the way count: a program that leaves them out, or rounds other values in their place, can miss the bound.
Values may be sent and summed in bfloat16 or wider, within the bound.
No kernel may reach another device: no remote copies, remote signals or barrier semaphores. Data moves between devices by JAX's collectives and lax.ppermute only.
A program may use at most 192 MiB of HBM per device.

v0:
```python
from functools import partial
import math
import jax
import jax.numpy as jnp
from jax import lax
from jax.sharding import PartitionSpec as P

D = 768
HEADS = 12
FF = 3072
beta_one = 0.9
beta_two = 0.999
adam_eps = 1e-06
decay_rate = 0.01
matrix_rate = 1.0
vector_rate = 0.3
clip_norm = 1.0
step_count = 10.0
norm_eps = 1e-06
masked_score = -1e30


def layer_norm(values, norm_gain, norm_shift):
    average = jnp.mean(values, axis=-1, keepdims=True)
    centered = values - average
    variance = jnp.mean(centered * centered, axis=-1, keepdims=True)
    return centered * lax.rsqrt(variance + norm_eps) * norm_gain + norm_shift


def split_vector(packed):
    bounds = [0, D, 2 * D, 2 * D + FF, 3 * D + FF, 4 * D + FF, 5 * D + FF, 6 * D + FF, 7 * D + FF]
    return [packed[bounds[place] : bounds[place + 1]] for place in range(8)]


def head_scores(query, keys, score_scale):
    return jnp.einsum("qhe,khe->hqk", query, keys, preferred_element_type=jnp.float32) * score_scale


def total_scores(pairs, score_scale):
    score_total = head_scores(pairs[0], pairs[1], score_scale)
    for place in range(2, len(pairs), 2):
        score_total = score_total + head_scores(pairs[place], pairs[place + 1], score_scale)
    return score_total


def attend_forward(block_item, score_scale):
    key_valid, value_rows = (block_item[0], block_item[1])
    score_total = total_scores(block_item[2:], score_scale)
    masked = jnp.where(key_valid[None, None, :], score_total, masked_score)
    row_max = jnp.max(masked, axis=-1, keepdims=True)
    exp_terms = jnp.exp(masked - row_max)
    row_sum = jnp.sum(exp_terms, axis=-1, keepdims=True)
    soft_low = (exp_terms / row_sum).astype(jnp.bfloat16)
    context = jnp.einsum("hqk,khe->qhe", soft_low, value_rows, preferred_element_type=jnp.float32)
    return (context.astype(jnp.bfloat16), (row_max + jnp.log(row_sum))[..., 0])


def attend_backward(block_item, score_scale, with_later, keep_total):
    key_valid, value_rows, log_norm, context_grad = (
        block_item[0],
        block_item[1],
        block_item[2],
        block_item[3],
    )
    rest = block_item[4:]
    if with_later:
        later = rest[0]
        pairs = rest[1:]
    else:
        pairs = rest
    score_total = total_scores(pairs, score_scale)
    soft = jnp.where(key_valid[None, None, :], jnp.exp(score_total - log_norm[..., None]), 0.0)
    soft_grad = jnp.einsum(
        "qhe,khe->hqk", context_grad, value_rows, preferred_element_type=jnp.float32
    )
    total_grad = soft * (soft_grad - jnp.sum(soft * soft_grad, axis=-1, keepdims=True))
    if with_later:
        total_grad = total_grad + later
    total_low = total_grad.astype(jnp.bfloat16)
    query_grad = (
        jnp.einsum("hqk,khe->qhe", total_low, pairs[1], preferred_element_type=jnp.float32)
        * score_scale
    )
    key_grad = (
        jnp.einsum("hqk,qhe->khe", total_low, pairs[0], preferred_element_type=jnp.float32)
        * score_scale
    )
    value_grad = jnp.einsum(
        "hqk,qhe->khe", soft.astype(jnp.bfloat16), context_grad, preferred_element_type=jnp.float32
    )
    results = (query_grad, key_grad, value_grad)
    if keep_total:
        results = results + (total_grad,)
    return results


def adam_parts(gradient, first, second, factor):
    clipped = gradient * factor
    first_new = beta_one * first + (1.0 - beta_one) * clipped
    second_new = beta_two * second + (1.0 - beta_two) * clipped * clipped
    first_hat = first_new / (1.0 - beta_one**step_count)
    second_hat = second_new / (1.0 - beta_two**step_count)
    return (first_new, second_new, first_hat / (jnp.sqrt(second_hat) + adam_eps))


def local(
    tokens,
    cotangent,
    lengths,
    proj_weight,
    out_weight,
    up_weight,
    down_weight,
    small_params,
    proj_first,
    proj_second,
    out_first,
    out_second,
    up_first,
    up_second,
    down_first,
    down_second,
    small_first,
    small_second,
):
    layers = proj_weight.shape[0]
    seq_count = lengths.shape[0]
    seq_len = tokens.shape[0] // seq_count
    local_width = proj_weight.shape[3]
    head_dim = D // HEADS
    local_heads = local_width // head_dim
    hidden_local = up_weight.shape[2]
    score_scale = 1.0 / math.sqrt(head_dim)
    share_scale = 1.0 / lax.axis_size("tensor")
    tensor_rank = lax.axis_index("tensor")
    proj_full, out_full, up_full, down_full = (
        lax.all_gather(proj_weight.astype(jnp.bfloat16), "dp", axis=1, tiled=True),
        lax.all_gather(out_weight.astype(jnp.bfloat16), "dp", axis=1, tiled=True),
        lax.all_gather(up_weight.astype(jnp.bfloat16), "dp", axis=1, tiled=True),
        lax.all_gather(down_weight.astype(jnp.bfloat16), "dp", axis=1, tiled=True),
    )
    positions = jnp.arange(seq_len)
    key_valid = positions[None, :] < lengths[:, None]
    row_valid = key_valid.reshape(-1, 1)

    def own_part(vector, width):
        return lax.dynamic_slice_in_dim(vector, tensor_rank * width, width)

    def place_part(local_values, full_width):
        return lax.dynamic_update_slice_in_dim(
            jnp.zeros((full_width,), jnp.float32),
            local_values,
            tensor_rank * local_values.shape[0],
            0,
        )

    def heads_view(rows):
        return rows.reshape(seq_count, seq_len, local_heads, head_dim)

    hidden = tokens.astype(jnp.float32)
    saved = []
    for layer_at in range(layers):
        bias_v, bias_o, bias_up, bias_down, gain_one, shift_one, gain_two, shift_two = split_vector(
            small_params[layer_at]
        )
        input_low = hidden.astype(jnp.bfloat16)
        projected = jnp.einsum(
            "td,dcf->tcf", input_low, proj_full[layer_at], preferred_element_type=jnp.float32
        )
        query_low = projected[:, 0].astype(jnp.bfloat16)
        key_low = projected[:, 1].astype(jnp.bfloat16)
        value_low = (projected[:, 2] + own_part(bias_v, local_width)).astype(jnp.bfloat16)
        pairs = [heads_view(query_low), heads_view(key_low)]
        for earlier in reversed(saved):
            pairs += [heads_view(earlier["query"]), heads_view(earlier["keys"])]
        context_low, log_norm = lax.map(
            partial(attend_forward, score_scale=score_scale),
            (key_valid, heads_view(value_low)) + tuple(pairs),
        )
        context_low = context_low.reshape(-1, local_width)
        attended = lax.psum(
            jnp.einsum(
                "tf,df->td", context_low, out_full[layer_at], preferred_element_type=jnp.float32
            ).astype(jnp.bfloat16),
            "tensor",
        ).astype(jnp.float32)
        first_in = hidden + attended + bias_o
        first_out = layer_norm(first_in, gain_one, shift_one)
        first_low = first_out.astype(jnp.bfloat16)
        before_act = jnp.einsum(
            "td,df->tf", first_low, up_full[layer_at], preferred_element_type=jnp.float32
        ) + own_part(bias_up, hidden_local)
        act_low = jax.nn.gelu(before_act, approximate=False).astype(jnp.bfloat16)
        returned = lax.psum(
            jnp.einsum(
                "tf,df->td", act_low, down_full[layer_at], preferred_element_type=jnp.float32
            ).astype(jnp.bfloat16),
            "tensor",
        ).astype(jnp.float32)
        second_in = first_out + returned + bias_down
        saved.append(
            {
                "layer_input": input_low,
                "query": query_low,
                "keys": key_low,
                "value_rows": value_low,
                "log_norm": log_norm,
                "context": context_low,
                "first_in": first_in,
                "first_low": first_low,
                "before_act": before_act,
                "act_low": act_low,
                "second_in": second_in,
            }
        )
        hidden = layer_norm(second_in, gain_two, shift_two)
    grad_rows = jnp.where(row_valid, cotangent.astype(jnp.float32), 0.0)
    proj_grads = [None] * layers
    out_grads = [None] * layers
    up_grads = [None] * layers
    down_grads = [None] * layers
    small_grads = [None] * layers
    later_total = None
    for layer_at in reversed(range(layers)):
        kept = saved[layer_at]
        bias_v, bias_o, bias_up, bias_down, gain_one, shift_one, gain_two, shift_two = split_vector(
            small_params[layer_at]
        )
        second_in_grad, gain_two_grad, shift_two_grad = jax.vjp(
            layer_norm, kept["second_in"], gain_two, shift_two
        )[1](grad_rows)
        down_in_low = second_in_grad.astype(jnp.bfloat16)
        down_grads[layer_at] = jnp.einsum(
            "td,tf->df", down_in_low, kept["act_low"], preferred_element_type=jnp.float32
        )
        act_grad = jnp.einsum(
            "td,df->tf", down_in_low, down_full[layer_at], preferred_element_type=jnp.float32
        )
        before_grad = jax.vjp(partial(jax.nn.gelu, approximate=False), kept["before_act"])[1](
            act_grad
        )[0]
        before_low = before_grad.astype(jnp.bfloat16)
        up_grads[layer_at] = jnp.einsum(
            "td,tf->df", kept["first_low"], before_low, preferred_element_type=jnp.float32
        )
        first_back = lax.psum(
            jnp.einsum(
                "tf,df->td", before_low, up_full[layer_at], preferred_element_type=jnp.float32
            ).astype(jnp.bfloat16),
            "tensor",
        ).astype(jnp.float32)
        first_out_grad = second_in_grad + first_back
        first_in_grad, gain_one_grad, shift_one_grad = jax.vjp(
            layer_norm, kept["first_in"], gain_one, shift_one
        )[1](first_out_grad)
        out_in_low = first_in_grad.astype(jnp.bfloat16)
        out_grads[layer_at] = jnp.einsum(
            "td,tf->df", out_in_low, kept["context"], preferred_element_type=jnp.float32
        )
        context_grad = jnp.einsum(
            "td,df->tf", out_in_low, out_full[layer_at], preferred_element_type=jnp.float32
        ).astype(jnp.bfloat16)
        pairs = [heads_view(kept["query"]), heads_view(kept["keys"])]
        for earlier in reversed(saved[:layer_at]):
            pairs += [heads_view(earlier["query"]), heads_view(earlier["keys"])]
        items = (
            key_valid,
            heads_view(kept["value_rows"]),
            kept["log_norm"],
            heads_view(context_grad),
        )
        with_later = later_total is not None
        if with_later:
            items = items + (later_total,)
        items = items + tuple(pairs)
        results = lax.map(
            partial(
                attend_backward,
                score_scale=score_scale,
                with_later=with_later,
                keep_total=layer_at > 0,
            ),
            items,
        )
        later_total = results[3] if layer_at > 0 else None
        query_grad = results[0].reshape(-1, local_width)
        key_grad = results[1].reshape(-1, local_width)
        value_grad = results[2].reshape(-1, local_width)
        proj_grad_low = jnp.stack([query_grad, key_grad, value_grad], axis=1).astype(jnp.bfloat16)
        proj_grads[layer_at] = jnp.einsum(
            "td,tcf->dcf", kept["layer_input"], proj_grad_low, preferred_element_type=jnp.float32
        )
        input_back = lax.psum(
            jnp.einsum(
                "tcf,dcf->td",
                proj_grad_low,
                proj_full[layer_at],
                preferred_element_type=jnp.float32,
            ).astype(jnp.bfloat16),
            "tensor",
        ).astype(jnp.float32)
        grad_rows = first_in_grad + input_back
        small_grads[layer_at] = jnp.concatenate(
            [
                place_part(jnp.sum(value_grad, axis=0), D),
                share_scale * jnp.sum(first_in_grad, axis=0),
                place_part(jnp.sum(before_grad, axis=0), FF),
                share_scale * jnp.sum(second_in_grad, axis=0),
                share_scale * gain_one_grad,
                share_scale * shift_one_grad,
                share_scale * gain_two_grad,
                share_scale * shift_two_grad,
            ]
        )
    big_totals = (
        jnp.stack(proj_grads),
        jnp.stack(out_grads),
        jnp.stack(up_grads),
        jnp.stack(down_grads),
    )
    small_partial = jnp.stack(small_grads)
    row_count = proj_weight.shape[1]
    summed = lax.psum((big_totals[0], big_totals[1], big_totals[2], big_totals[3]), "dp")
    row_start = lax.axis_index("dp") * row_count
    shares = tuple(
        (lax.dynamic_slice_in_dim(summed_part, row_start, row_count, 1) for summed_part in summed)
    )
    masters = (proj_weight, out_weight, up_weight, down_weight)
    firsts = (proj_first, out_first, up_first, down_first)
    seconds = (proj_second, out_second, up_second, down_second)
    square_part = jnp.sum(shares[0] * shares[0])
    for kind_at in range(1, 4):
        square_part = square_part + jnp.sum(shares[kind_at] * shares[kind_at])
    weight_square = jnp.stack(
        [jnp.sum(master * master, axis=tuple(range(1, master.ndim))) for master in masters]
    )
    square_big, weight_square, small_grad = lax.psum(
        (square_part, weight_square, small_partial), ("dp", "tensor")
    )
    grad_norm = jnp.sqrt(square_big + jnp.sum(small_grad * small_grad))
    factor = clip_norm / jnp.maximum(grad_norm, clip_norm)
    moments = []
    updates = []
    for kind_at in range(4):
        first_new, second_new, direction = adam_parts(
            shares[kind_at], firsts[kind_at], seconds[kind_at], factor
        )
        moments.append((first_new, second_new))
        updates.append(direction + decay_rate * masters[kind_at])
    update_square = jnp.stack(
        [jnp.sum(update * update, axis=tuple(range(1, update.ndim))) for update in updates]
    )
    update_square = lax.psum(update_square, ("dp", "tensor"))
    ratio = jnp.sqrt(weight_square) / jnp.sqrt(update_square)
    outputs = [hidden, grad_rows, grad_norm]
    for kind_at in range(4):
        master = masters[kind_at]
        scaled = ratio[kind_at].reshape((-1,) + (1,) * (master.ndim - 1))
        outputs += [
            moments[kind_at][0],
            moments[kind_at][1],
            master - matrix_rate * scaled * updates[kind_at],
        ]
    small_first_new, small_second_new, small_direction = adam_parts(
        small_grad, small_first, small_second, factor
    )
    outputs += [small_first_new, small_second_new, small_params - vector_rate * small_direction]
    return tuple(outputs)


def solution(mesh):
    placed = (
        P("dp", None),
        P("dp", None),
        P("dp"),
        P(None, "dp", None, "tensor"),
        P(None, "dp", "tensor"),
        P(None, "dp", "tensor"),
        P(None, "dp", "tensor"),
        P(),
        P(None, "dp", None, "tensor"),
        P(None, "dp", None, "tensor"),
        P(None, "dp", "tensor"),
        P(None, "dp", "tensor"),
        P(None, "dp", "tensor"),
        P(None, "dp", "tensor"),
        P(None, "dp", "tensor"),
        P(None, "dp", "tensor"),
        P(),
        P(),
    )
    return jax.shard_map(
        local,
        mesh=mesh,
        in_specs=placed,
        out_specs=(
            P("dp", None),
            P("dp", None),
            P(),
            P(None, "dp", None, "tensor"),
            P(None, "dp", None, "tensor"),
            P(None, "dp", None, "tensor"),
            P(None, "dp", "tensor"),
            P(None, "dp", "tensor"),
            P(None, "dp", "tensor"),
            P(None, "dp", "tensor"),
            P(None, "dp", "tensor"),
            P(None, "dp", "tensor"),
            P(None, "dp", "tensor"),
            P(None, "dp", "tensor"),
            P(None, "dp", "tensor"),
            P(),
            P(),
            P(),
        ),
        check_vma=False,
    )
```

profile of v0, /device:TPU:0, one launch (start us, length us, event | category | flops | bytes accessed | tf_op | source)
XLA Modules:
  0.0 1741.2 jit_solution(10675762374318251473)
XLA Ops:
  13.1 72.2 %all-gather.5.cloned.1.call-done = bf16[2,768,3,384]{3,1,2,0:T(8,128)(2,1)} async-done(((bf16[2,48,3,384]{3,1,2,0:T(8,128)(2,1)}), bf16[2,768,3,384]{3,1,2,0:T(8,128)(2,1)}) %all-gather.5.cloned.1.call-update) | async-done | bytes 3538960 | tf_op jit(solution)/shard_map/all_gather | solution.py:137
  85.3 5.6 fusion.209
  103.5 11.4 while.54
  116.8 26.5 %all-gather.7.cloned.1.call-done = bf16[2,768,384]{2,1,0:T(8,128)(2,1)} async-done(((bf16[2,48,384]{2,1,0:T(8,128)(2,1)}), bf16[2,768,384]{2,1,0:T(8,128)(2,1)}) %all-gather.7.cloned.1.call-update) | async-done | bytes 1179664 | tf_op jit(solution)/shard_map/all_gather | solution.py:138
  150.6 15.8 all-reduce.13.cloned.1.call-done
  169.4 82.1 %all-gather.9.cloned.1.call-done = bf16[2,768,1536]{2,1,0:T(8,128)(2,1)} async-done(((bf16[2,48,1536]{2,1,0:T(8,128)(2,1)}), bf16[2,768,1536]{2,1,0:T(8,128)(2,1)}) %all-gather.9.cloned.1.call-update) | async-done | bytes 4718608 | tf_op jit(solution)/shard_map/all_gather | solution.py:139
  251.5 20.8 %multiply_convert_fusion.1 = (bf16[1024,1536]{1,0:T(8,128)(2,1)}, f32[1024,1536]{1,0:T(8,128)}, f32[1024,1536]{1,0:T(8,128)}) fusion(f32[1536]{0:T(1024)S(1)} %dynamic-slice_reduce_fusion.5, bf16[2,768,1536]{2,1,0:T(8,128)(2,1)} %all-gather.9.cloned.1.call-done, f32[768]{0:T(1024)S(1)} %get-tuple-element.431, f32[768]{0:T(1024)S(1)} %get-tuple-element.432, ...), kind=kOutput, calls=%fused_computation.155 | convolution fusion | flops 2526806016 | bytes 21257216 | tf_op jit(solution)/shard_map/td,df->tf/dot_general | solution.py:190
  272.3 61.6 %all-gather.11.cloned.1.call-done = bf16[2,768,1536]{2,1,0:T(8,128)(2,1)} async-done(((bf16[2,48,1536]{2,1,0:T(8,128)(2,1)}), bf16[2,768,1536]{2,1,0:T(8,128)(2,1)}) %all-gather.11.cloned.1.call-update) | async-done | bytes 4718608 | tf_op jit(solution)/shard_map/all_gather | solution.py:140
  333.9 6.4 fusion.151
  340.5 19.1 %all-reduce.15.cloned.1.call-done = bf16[1024,768]{1,0:T(8,128)(2,1)} async-done(((bf16[1024,768]{1,0:T(8,128)(2,1)}), bf16[1024,768]{1,0:T(8,128)(2,1)}) %all-reduce.15.cloned.1.call-update) | async-done | bytes 1572880 | tf_op jit(solution)/shard_map/psum | solution.py:194
  363.7 3.8 fusion.210
  380.8 14.3 while.55
  400.4 21.7 %all-reduce.17.cloned.1.call-done = bf16[1024,768]{1,0:T(8,128)(2,1)} async-done(((bf16[1024,768]{1,0:T(8,128)(2,1)}), bf16[1024,768]{1,0:T(8,128)(2,1)}) %all-reduce.17.cloned.1.call-update) | async-done | bytes 1572880 | tf_op jit(solution)/shard_map/psum | solution.py:181
  426.5 18.6 %multiply_convert_fusion = (bf16[1024,1536]{1,0:T(8,128)(2,1)S(1)}, f32[1024,1536]{1,0:T(8,128)}, f32[1024,1536]{1,0:T(8,128)}) fusion(f32[1536]{0:T(1024)S(1)} %dynamic-slice_reduce_fusion.4, bf16[2,768,1536]{2,1,0:T(8,128)(2,1)S(1)} %bitcast.417, f32[1024,768]{1,0:T(8,128)S(1)} %get-tuple-element.545, f32[768]{0:T(1024)S(1)} %copy-done.104, ...), kind=kOutput, calls=%fused_computation.142 | convolution fusion | flops 2523660288 | bytes 21258240 | tf_op jit(solution)/shard_map/td,df->tf/dot_general | solution.py:190
  446.8 5.4 fusion.149
  452.2 21.7 %all-reduce.19.cloned.1.call-done = bf16[1024,768]{1,0:T(8,128)(2,1)} async-done(((bf16[1024,768]{1,0:T(8,128)(2,1)}), bf16[1024,768]{1,0:T(8,128)(2,1)}) %all-reduce.19.cloned.1.call-update) | async-done | bytes 1572880 | tf_op jit(solution)/shard_map/psum | solution.py:194
  484.4 9.5 fusion.211
  495.6 3.7 fusion.150
  503.6 8.0 convolution_bitcast_fusion.2
  511.6 9.5 all-reduce.21.cloned.1.call-done
  521.1 4.9 multiply_reduce_fusion.3
  541.2 36.4 %while.56 = (s32[]{:T(128)}, bf16[2,512,6,64]{1,3,2,0:T(8,128)(2,1)}, bf16[2,512,6,64]{1,3,2,0:T(8,128)(2,1)}, f32[2,512,6,64]{1,3,2,0:T(8,128)}, f32[2,6,512,51...) while((s32[]{:T(128)}, ...), condition=%wide.region_27.28_spmd, body=%wide.region_25.27_spmd.sunk | while | flops 1227224064 | bytes 94064864 | solution.py:276
  548.1 4.2 bitcast_dynamic-update-slice_fusion.8
  566.1 4.3 bitcast_dynamic-update-slice_fusion.8
  592.2 5.6 bitcast_convert_fusion.1
  598.0 7.9 convolution_bitcast_fusion
  608.8 4.3 convolution_bitcast_fusion.4
  613.1 6.5 all-reduce.23.cloned.1.call-done
  619.7 5.1 multiply_reduce_fusion.4
  627.1 9.6 fusion.212
  638.3 3.7 fusion.152
  642.1 5.6 convolution_bitcast_fusion.1
  647.8 7.4 pad_maximum_fusion.1
  655.3 4.9 convolution_bitcast_fusion.3
  663.8 4.8 multiply_reduce_fusion.5
  676.7 54.2 %while.57 = (s32[]{:T(128)}, bf16[2,512,6,64]{1,3,2,0:T(8,128)(2,1)}, bf16[2,512,6,64]{1,3,2,0:T(8,128)(2,1)}, f32[2,512,6,64]{1,3,2,0:T(8,128)}, bf16[2,512,6,6...) while((s32[]{:T(128)}, ...), condition=%wide.region_36.37_spmd, body=%wide.region_34.36_spmd.sunk | while | flops 1222512128 | bytes 87736576 | solution.py:276
  676.7 5.2 exponential_select_fusion.3
  681.9 7.6 fusion.310
  689.5 7.8 fusion.311
  703.8 5.2 exponential_select_fusion.3
  709.0 7.6 fusion.310
  716.6 7.8 fusion.311
  739.8 5.2 bitcast_convert_fusion
  745.3 8.5 pad_maximum_fusion
  772.1 736.8 %all-reduce.31.cloned.1.call-done = (f32[2,768,3,384]{3,1,2,0:T(8,128)}, f32[2,768,384]{2,1,0:T(8,128)}, f32[2,768,1536]{2,1,0:T(8,128)}, f32[2,768,1536]{2,1,0:T(8,128)}) async-done(((f32[2,768,3,384]{3,1,2,0:T(8,128)}, f32[2,768,384]{2,1,0:T(8,128)}, f32[2,768,1536]{2,1,0:T(8,128)}, f32[2,768,1536]{2,1,0:T(8,128)}), (f32[2,768,3,384]{3,1,2,0:T(8,128)}, f32[2,768,384]{2,1,0:T(8,128)}, ...) | async-done | bytes 28311568 | tf_op jit(solution)/shard_map/psum | solution.py:323
  1518.5 114.0 %all-reduce.29.cloned.1.call-done = f32[2,8448]{1,0:T(2,128)} async-done(((f32[2,8448]{1,0:T(2,128)}), f32[2,8448]{1,0:T(2,128)}) %all-reduce.29.cloned.1.call-update) | async-done | bytes 67600 | tf_op jit(solution)/shard_map/psum | solution.py:337
  1634.1 42.6 %psum.124 = f32[]{:T(128)} all-reduce(f32[]{:T(128)S(6)} %add.424), channel_id=1, replica_groups=mesh['dp'=16,'tensor'=2] {'dp','tensor'}, use_global_device_ids=true, to_apply=%region_46.47 | all-reduce | flops 1 | bytes 8 | tf_op jit(solution)/shard_map/psum | solution.py:337
  1687.8 39.3 %all-reduce = (f32[4,2]{1,0:T(4,128)S(1)}, f32[4,2]{1,0:T(4,128)S(1)}) all-reduce(f32[4,2]{1,0:T(4,128)S(1)} %pad_maximum_fusion.12, f32[4,2]{1,0:T(4,128)S(1)} %pad_maximum_fusion.11), channel_id=1, replica_groups=mesh['dp'=16,'tensor'=2] {'dp','tensor'}, use_global_device_ids=true, to_apply=%region_74.75 | all-reduce | flops 16 | bytes 128 | tf_op jit(solution)/shard_map/psum | solution.py:353
  (542 shorter events, 240.5 us)
Async XLA Ops:
  7.2 78.1 %all-gather.5.cloned.1.call-start = ((), (), s32[]{:S(2)}) async-start(), calls=%async_computation | async-start | bytes 3760128 | tf_op jit(solution)/shard_map/all_gather | solution.py:137
  9.0 134.3 %all-gather.7.cloned.1.call-start = ((), (), s32[]{:S(2)}) async-start(), calls=%async_computation.1 | async-start | bytes 1253376 | tf_op jit(solution)/shard_map/all_gather | solution.py:138
  10.6 155.7 %all-reduce.13.cloned.1.call-start = ((), (), s32[]{:S(2)}) async-start(), calls=%async_computation.2 | async-start | bytes 3145728 | tf_op jit(solution)/shard_map/psum | solution.py:181
  12.2 347.3 %copy-start.73 = (f32[768]{0:T(1024)}, f32[768]{0:T(1024)S(1)}, u32[]{:S(2)}) copy-start(f32[768]{0:T(1024)S(1)} %get-tuple-element.433) | copy-start | bytes 9220
  12.2 347.3 %copy-start.82 = (f32[768]{0:T(1024)}, f32[768]{0:T(1024)S(1)}, u32[]{:S(2)}) copy-start(f32[768]{0:T(1024)S(1)} %get-tuple-element.432) | copy-start | bytes 9220
  12.2 347.3 %copy-start.100 = (f32[768]{0:T(1024)}, f32[768]{0:T(1024)S(1)}, u32[]{:S(2)}) copy-start(f32[768]{0:T(1024)S(1)} %get-tuple-element.431) | copy-start | bytes 9220
  12.2 409.8 %copy-start.86 = (f32[768]{0:T(1024)}, f32[768]{0:T(1024)S(1)}, u32[]{:S(2)}) copy-start(f32[768]{0:T(1024)S(1)} %get-tuple-element.429) | copy-start | bytes 9220
  12.2 409.8 %copy-start.102 = (f32[768]{0:T(1024)}, f32[768]{0:T(1024)S(1)}, u32[]{:S(2)}) copy-start(f32[768]{0:T(1024)S(1)} %get-tuple-element.428) | copy-start | bytes 9220
  114.9 28.3 %copy-start.20 = (bf16[2,512,6,64]{1,3,2,0:T(8,128)(2,1)}, bf16[2,512,6,64]{1,3,2,0:T(8,128)(2,1)S(1)}, u32[]{:S(2)}) copy-start(bf16[2,512,6,64]{1,3,2,0:T(8,128)(2,1)S(1)} %get-tuple-element.1014) | copy-start | bytes 2359300
  114.9 31.9 %copy-start.69 = (f32[2,6,512]{2,1,0:T(8,128)}, f32[2,6,512]{2,1,0:T(8,128)S(1)}, u32[]{:S(2)}) copy-start(f32[2,6,512]{2,1,0:T(8,128)S(1)} %get-tuple-element.954) | copy-start | bytes 73732
  116.8 32.0 %copy-start.32 = (f32[2,48,1536]{2,1,0:T(8,128)S(1)}, f32[2,48,1536]{2,1,0:T(8,128)}, u32[]{:S(2)}) copy-start(f32[2,48,1536]{2,1,0:T(8,128)} %param.32) | copy-start | bytes 1769476
  143.3 23.1 %copy-start.10 = (bf16[1024,768]{1,0:T(8,128)(2,1)S(1)}, bf16[1024,768]{1,0:T(8,128)(2,1)}, u32[]{:S(2)}) copy-start(bf16[1024,768]{1,0:T(8,128)(2,1)} %param.26) | copy-start | bytes 4718596
  146.9 104.6 %all-gather.9.cloned.1.call-start = ((), (), s32[]{:S(2)}) async-start(), calls=%async_computation.3 | async-start | bytes 5013504 | tf_op jit(solution)/shard_map/all_gather | solution.py:139
  148.8 185.2 %all-gather.11.cloned.1.call-start = ((), (), s32[]{:S(2)}) async-start(), calls=%async_computation.4 | async-start | bytes 5013504 | tf_op jit(solution)/shard_map/all_gather | solution.py:140
  149.6 209.9 %all-reduce.15.cloned.1.call-start = ((), (), s32[]{:S(2)}) async-start(), calls=%async_computation.5 | async-start | bytes 3145728 | tf_op jit(solution)/shard_map/psum | solution.py:194
  150.5 100.9 %copy-start.116 = (f32[1536]{0:T(1024)}, f32[1536]{0:T(1024)S(1)}, u32[]{:S(2)}) copy-start(f32[1536]{0:T(1024)S(1)} %dynamic-slice_reduce_fusion.5) | copy-start | bytes 18436
  168.5 191.1 %copy-start.76 = (f32[1024]{0:T(1024)}, f32[1024]{0:T(1024)S(1)}, u32[]{:S(2)}) copy-start(f32[1024]{0:T(1024)S(1)} %broadcast_multiply_fusion.3) | copy-start | bytes 12292
  169.4 102.9 %copy-start.92 = (f32[1024]{0:T(1024)}, f32[1024]{0:T(1024)S(1)}, u32[]{:S(2)}) copy-start(f32[1024]{0:T(1024)S(1)} %multiply_reduce_fusion.13) | copy-start | bytes 12292
  169.4 190.2 %copy-start.84 = (f32[1024]{0:T(1024)}, f32[1024]{0:T(1024)S(1)}, u32[]{:S(2)}) copy-start(f32[1024]{0:T(1024)S(1)} %fusion.167) | copy-start | bytes 12292
  340.4 81.7 %all-reduce.17.cloned.1.call-start = ((), (), s32[]{:S(2)}) async-start(), calls=%async_computation.6 | async-start | bytes 3145728 | tf_op jit(solution)/shard_map/psum | solution.py:181
  363.2 58.9 %copy-start.78 = (f32[1024]{0:T(1024)}, f32[1024]{0:T(1024)S(1)}, u32[]{:S(2)}) copy-start(f32[1024]{0:T(1024)S(1)} %broadcast_multiply_fusion.2) | copy-start | bytes 12292
  363.7 58.4 %copy-start.89 = (f32[1024]{0:T(1024)}, f32[1024]{0:T(1024)S(1)}, u32[]{:S(2)}) copy-start(f32[1024]{0:T(1024)S(1)} %fusion.168) | copy-start | bytes 12292
  397.1 25.0 %copy-start.106 = (f32[768]{0:T(1024)S(1)}, f32[768]{0:T(1024)}, u32[]{:S(2)}) copy-start(f32[768]{0:T(1024)} %get-tuple-element.427) | copy-start | bytes 9220
  400.3 73.6 %all-reduce.19.cloned.1.call-start = ((), (), s32[]{:S(2)}) async-start(), calls=%async_computation.7 | async-start | bytes 3145728 | tf_op jit(solution)/shard_map/psum | solution.py:194
  425.8 19.4 %copy-start.3 = (f32[1024,768]{1,0:T(8,128)}, f32[1024,768]{1,0:T(8,128)S(1)}, u32[]{:S(2)}) copy-start(f32[1024,768]{1,0:T(8,128)S(1)} %get-tuple-element.545) | copy-start | bytes 9437188
  446.8 27.2 %copy-start.105 = (f32[768]{0:T(1024)S(1)}, f32[768]{0:T(1024)}, u32[]{:S(2)}) copy-start(f32[768]{0:T(1024)} %get-tuple-element.424) | copy-start | bytes 9220
  452.2 68.9 %all-reduce.21.cloned.1.call-start = ((), (), s32[]{:S(2)}) async-start(), calls=%async_computation.8 | async-start | bytes 3145728 | tf_op jit(solution)/shard_map/psum | solution.py:246
  481.4 14.2 slice-start.4
  484.4 11.2 slice-start.5
  499.3 120.3 %all-reduce.23.cloned.1.call-start = ((), (), s32[]{:S(2)}) async-start(), calls=%async_computation.9 | async-start | bytes 3145728 | tf_op jit(solution)/shard_map/psum | solution.py:293
  597.9 65.9 %all-reduce.25.cloned.1.call-start = ((), (), s32[]{:S(2)}) async-start(), calls=%async_computation.10 | async-start | bytes 3145728 | tf_op jit(solution)/shard_map/psum | solution.py:246
  613.1 11.7 copy-start.95
  625.2 13.1 slice-start.6
  627.1 11.3 slice-start.7
  642.1 125.4 %all-reduce.27.cloned.1.call-start = ((), (), s32[]{:S(2)}) async-start(), calls=%async_computation.11 | async-start | bytes 3145728 | tf_op jit(solution)/shard_map/psum | solution.py:293
  681.9 19.8 %slice-start = ((s8[6291456]{0:T(1024)(128)(4,1)}), s8[2097152]{0:T(1024)(128)(4,1)S(1)}, s32[]{:S(2)}) async-start(s8[6291456]{0:T(1024)(128)(4,1)} %bitcast.400), calls=%async_computation.14 | async-start | bytes 4194304 | tf_op jit(solution)/shard_map/while
  689.5 12.2 slice-start.1
  709.0 19.8 %slice-start = ((s8[6291456]{0:T(1024)(128)(4,1)}), s8[2097152]{0:T(1024)(128)(4,1)S(1)}, s32[]{:S(2)}) async-start(s8[6291456]{0:T(1024)(128)(4,1)} %bitcast.400), calls=%async_computation.14 | async-start | bytes 4194304 | tf_op jit(solution)/shard_map/while
  716.6 12.2 slice-start.1
  745.0 763.9 %all-reduce.31.cloned.1.call-start = ((), (), s32[]{:S(2)}) async-start(), calls=%async_computation.13 | async-start | bytes 56623104 | tf_op jit(solution)/shard_map/psum | solution.py:323
  763.9 868.6 %all-reduce.29.cloned.1.call-start = ((), (), s32[]{:S(2)}) async-start(), calls=%async_computation.12 | async-start | bytes 135168 | tf_op jit(solution)/shard_map/psum | solution.py:337
  767.5 910.6 %copy-start.47 = (f32[2,48,384]{2,1,0:T(8,128)S(1)}, f32[2,48,384]{2,1,0:T(8,128)}, u32[]{:S(2)}) copy-start(f32[2,48,384]{2,1,0:T(8,128)} %param.30) | copy-start | bytes 442372
  771.2 908.8 %copy-start.34 = (f32[2,48,1536]{2,1,0:T(8,128)S(1)}, f32[2,48,1536]{2,1,0:T(8,128)}, u32[]{:S(2)}) copy-start(f32[2,48,1536]{2,1,0:T(8,128)} %param.31) | copy-start | bytes 1769476
  771.2 908.8 %copy-start.66 = (f32[2,48,1536]{2,1,0:T(8,128)S(1)}, f32[2,48,1536]{2,1,0:T(8,128)}, u32[]{:S(2)}) copy-start(f32[2,48,1536]{2,1,0:T(8,128)} %param.38) | copy-start | bytes 1769476
  1508.9 173.1 %copy-start.33 = (f32[2,48,1536]{2,1,0:T(8,128)S(1)}, f32[2,48,1536]{2,1,0:T(8,128)}, u32[]{:S(2)}) copy-start(f32[2,48,1536]{2,1,0:T(8,128)} %param.32) | copy-start | bytes 1769476
  1682.0 47.4 %copy-start.42 = (f32[2,48,1536]{2,1,0:T(8,128)}, f32[2,48,1536]{2,1,0:T(8,128)S(1)}, u32[]{:S(2)}) copy-start(f32[2,48,1536]{2,1,0:T(8,128)S(1)} %get-tuple-element.528) | copy-start | bytes 1769476
  1682.0 47.4 %copy-start.43 = (f32[2,48,1536]{2,1,0:T(8,128)}, f32[2,48,1536]{2,1,0:T(8,128)S(1)}, u32[]{:S(2)}) copy-start(f32[2,48,1536]{2,1,0:T(8,128)S(1)} %get-tuple-element.529) | copy-start | bytes 1769476
  1685.2 45.4 %copy-start.44 = (f32[2,48,1536]{2,1,0:T(8,128)}, f32[2,48,1536]{2,1,0:T(8,128)S(1)}, u32[]{:S(2)}) copy-start(f32[2,48,1536]{2,1,0:T(8,128)S(1)} %get-tuple-element.530) | copy-start | bytes 1769476
  (111 other events, 434.2 us)
Sparse Core Ops, SparseCore 0:
  11.3 73.9 all-gather.4
  88.5 54.6 all-gather.6
  147.0 19.2 all-reduce.12
  169.8 81.6 all-gather.8
  255.0 78.9 all-gather.10
  340.5 19.0 all-reduce.14
  400.5 21.5 all-reduce.16
  452.3 21.5 all-reduce.18
  499.5 21.5 all-reduce.20
  598.0 21.5 all-reduce.22
  642.2 21.5 all-reduce.24
  745.1 21.5 all-reduce.26
  773.2 735.7 all-reduce.30
  1515.9 116.6 all-reduce.28
where the time goes:
time: 1750 us; the launch traced here: 1740 us
  waiting for transfers between devices  1190 us (68%)
  matrix products  238 us (14%)
  other arithmetic  120 us (7%)
  local copies, waits for them, and re-layouts  86.9 us (5%)
  blocking collectives  81.9 us (5%)
  between operations  20.9 us (1%)
    psum x1, waiting for transfers between devices, local(): lax.psum((big_totals[0], big_totals[1], big_totals[2], big_totals[3]), 'dp')  737 us
    psum x1, waiting for transfers between devices, local(): lax.psum((square_part, weight_square, small_partial), ('dp', 'tensor'))  114 us
    all_gather x1, waiting for transfers between devices, local(): lax.all_gather(up_weight.astype(jnp.bfloat16), 'dp', axis=1, tiled=True)  82.1 us
    all_gather x1, waiting for transfers between devices, local(): lax.all_gather(proj_weight.astype(jnp.bfloat16), 'dp', axis=1, tiled=True)  72.2 us
    all_gather x1, waiting for transfers between devices, local(): lax.all_gather(down_weight.astype(jnp.bfloat16), 'dp', axis=1, tiled=True)  61.6 us
    psum x1, blocking collectives, local(): lax.psum((square_part, weight_square, small_partial), ('dp', 'tensor'))  42.6 us
    psum x2, waiting for transfers between devices, local(): lax.psum(jnp.einsum('tf,df->td', act_low, down_full[layer_at], preferred_...  40.7 us
    dot_general x2, matrix products, local(): jnp.einsum('td,df->tf', first_low, up_full[layer_at], preferred_element_t...  39.4 us
  transfers between devices with their start and end apart: 14, of which 13 were waited for; matrix products, arithmetic and copies ran while one was open for 8% of the time, Pallas kernels for 0%

commit v1 on v0

--- a/solution.py
+++ b/solution.py
@@ -350,7 +350,7 @@
     update_square = jnp.stack(
         [jnp.sum(update * update, axis=tuple(range(1, update.ndim))) for update in updates]
     )
-    update_square = lax.psum(update_square, ("dp", "tensor"))
+    update_square = jnp.sum(lax.all_gather(update_square, ("dp", "tensor")), axis=0)
     ratio = jnp.sqrt(weight_square) / jnp.sqrt(update_square)
     outputs = [hidden, grad_rows, grad_norm]
     for kind_at in range(4):

time: 1750 us -> 1780 us (1.017)
  blocking collectives: 81.9 us -> 123 us
    all_gather x0 -> x1, blocking collectives: none -> 41.2 us  [local(): lax.all_gather(update_square, ('dp', 'tensor'))]
    psum x1 -> x0, blocking collectives: 39.3 us -> none  [local(): update_square = lax.psum(update_square, ('dp', 'tensor'))]
    psum x1 -> x2, blocking collectives: 42.6 us -> 81.8 us  [local(): lax.psum((square_part, weight_square, small_partial), ('dp', 'tensor'))]
  transfers between devices with their start and end apart: 14 -> 14, of which waited for: 13 -> 14; matrix products, arithmetic and copies ran while one was open for 8% -> 7% of each run, Pallas kernels for 0% -> 0%
where the time goes in v1:
time: 1780 us; the launch traced here: 1770 us
  waiting for transfers between devices  1200 us (67%)
  matrix products  237 us (13%)
  blocking collectives  123 us (7%)
  other arithmetic  120 us (7%)
  local copies, waits for them, and re-layouts  72.9 us (4%)
  between operations  20.9 us (1%)
    psum x1, waiting for transfers between devices, local(): lax.psum((big_totals[0], big_totals[1], big_totals[2], big_totals[3]), 'dp')  737 us
    psum x1, waiting for transfers between devices, local(): lax.psum((square_part, weight_square, small_partial), ('dp', 'tensor'))  114 us
    all_gather x1, waiting for transfers between devices, local(): lax.all_gather(up_weight.astype(jnp.bfloat16), 'dp', axis=1, tiled=True)  82.1 us
    psum x2, blocking collectives, local(): lax.psum((square_part, weight_square, small_partial), ('dp', 'tensor'))  81.8 us
    all_gather x1, waiting for transfers between devices, local(): lax.all_gather(proj_weight.astype(jnp.bfloat16), 'dp', axis=1, tiled=True)  71.6 us
    all_gather x1, waiting for transfers between devices, local(): lax.all_gather(down_weight.astype(jnp.bfloat16), 'dp', axis=1, tiled=True)  62 us
    all_gather x1, blocking collectives, local(): lax.all_gather(update_square, ('dp', 'tensor'))  41.2 us
    psum x2, waiting for transfers between devices, local(): lax.psum(jnp.einsum('tf,df->td', act_low, down_full[layer_at], preferred_...  40.5 us
  transfers between devices with their start and end apart: 14, of which 14 were waited for; matrix products, arithmetic and copies ran while one was open for 7% of the time, Pallas kernels for 0%

profile of v1, /device:TPU:0, one launch (start us, length us, event | category | flops | bytes accessed | tf_op | source)
XLA Modules:
  0.0 1774.6 jit_solution(389258067271844284)
XLA Ops:
  13.7 71.6 %all-gather.7.cloned.1.call-done = bf16[2,768,3,384]{3,1,2,0:T(8,128)(2,1)} async-done(((bf16[2,48,3,384]{3,1,2,0:T(8,128)(2,1)}), bf16[2,768,3,384]{3,1,2,0:T(8,128)(2,1)}) %all-gather.7.cloned.1.call-update) | async-done | bytes 3538960 | tf_op jit(solution)/shard_map/all_gather | solution.py:137
  85.3 5.6 fusion.209
  100.1 11.4 while.54
  113.4 29.9 %all-gather.9.cloned.1.call-done = bf16[2,768,384]{2,1,0:T(8,128)(2,1)} async-done(((bf16[2,48,384]{2,1,0:T(8,128)(2,1)}), bf16[2,768,384]{2,1,0:T(8,128)(2,1)}) %all-gather.9.cloned.1.call-update) | async-done | bytes 1179664 | tf_op jit(solution)/shard_map/all_gather | solution.py:138
  149.7 16.6 all-reduce.12.cloned.1.call-done
  169.4 82.1 %all-gather.11.cloned.1.call-done = bf16[2,768,1536]{2,1,0:T(8,128)(2,1)} async-done(((bf16[2,48,1536]{2,1,0:T(8,128)(2,1)}), bf16[2,768,1536]{2,1,0:T(8,128)(2,1)}) %all-gather.11.cloned.1.call-update) | async-done | bytes 4718608 | tf_op jit(solution)/shard_map/all_gather | solution.py:139
  251.5 20.6 %multiply_convert_fusion.1 = (bf16[1024,1536]{1,0:T(8,128)(2,1)}, f32[1024,1536]{1,0:T(8,128)}, f32[1024,1536]{1,0:T(8,128)}) fusion(f32[1536]{0:T(1024)S(1)} %dynamic-slice_reduce_fusion.5, bf16[2,768,1536]{2,1,0:T(8,128)(2,1)} %all-gather.11.cloned.1.call-done, f32[768]{0:T(1024)S(1)} %copy-done.88, f32[768]{0:T(1024)S(1)} %get-tuple-element.548, ...), kind=kOutput, calls=%fused_computation.155 | convolution fusion | flops 2526806016 | bytes 21257216 | tf_op jit(solution)/shard_map/td,df->tf/dot_general | solution.py:190
  272.1 62.0 %all-gather.13.cloned.1.call-done = bf16[2,768,1536]{2,1,0:T(8,128)(2,1)} async-done(((bf16[2,48,1536]{2,1,0:T(8,128)(2,1)}), bf16[2,768,1536]{2,1,0:T(8,128)(2,1)}) %all-gather.13.cloned.1.call-update) | async-done | bytes 4718608 | tf_op jit(solution)/shard_map/all_gather | solution.py:140
  334.1 6.4 fusion.151
  340.9 18.8 %all-reduce.14.cloned.1.call-done = bf16[1024,768]{1,0:T(8,128)(2,1)} async-done(((bf16[1024,768]{1,0:T(8,128)(2,1)}), bf16[1024,768]{1,0:T(8,128)(2,1)}) %all-reduce.14.cloned.1.call-update) | async-done | bytes 1572880 | tf_op jit(solution)/shard_map/psum | solution.py:194
  363.8 3.8 fusion.210
  380.8 13.8 while.55
  400.2 21.6 %all-reduce.16.cloned.1.call-done = bf16[1024,768]{1,0:T(8,128)(2,1)} async-done(((bf16[1024,768]{1,0:T(8,128)(2,1)}), bf16[1024,768]{1,0:T(8,128)(2,1)}) %all-reduce.16.cloned.1.call-update) | async-done | bytes 1572880 | tf_op jit(solution)/shard_map/psum | solution.py:181
  426.3 18.7 %multiply_convert_fusion = (bf16[1024,1536]{1,0:T(8,128)(2,1)S(1)}, f32[1024,1536]{1,0:T(8,128)}, f32[1024,1536]{1,0:T(8,128)}) fusion(f32[1536]{0:T(1024)S(1)} %dynamic-slice_reduce_fusion.4, bf16[2,768,1536]{2,1,0:T(8,128)(2,1)S(1)} %bitcast.411, f32[1024,768]{1,0:T(8,128)S(1)} %get-tuple-element.663, f32[768]{0:T(1024)S(1)} %copy-done.92, ...), kind=kOutput, calls=%fused_computation.142 | convolution fusion | flops 2523660288 | bytes 21258240 | tf_op jit(solution)/shard_map/td,df->tf/dot_general | solution.py:190
  446.7 5.4 fusion.149
  452.1 21.7 %all-reduce.18.cloned.1.call-done = bf16[1024,768]{1,0:T(8,128)(2,1)} async-done(((bf16[1024,768]{1,0:T(8,128)(2,1)}), bf16[1024,768]{1,0:T(8,128)(2,1)}) %all-reduce.18.cloned.1.call-update) | async-done | bytes 1572880 | tf_op jit(solution)/shard_map/psum | solution.py:194
  484.3 9.5 fusion.211
  502.1 8.0 convolution_bitcast_fusion.2
  510.1 10.9 all-reduce.20.cloned.1.call-done
  521.0 4.9 multiply_reduce_fusion.3
  537.5 36.2 %while.56 = (s32[]{:T(128)}, bf16[2,512,6,64]{1,3,2,0:T(8,128)(2,1)}, bf16[2,512,6,64]{1,3,2,0:T(8,128)(2,1)}, f32[2,512,6,64]{1,3,2,0:T(8,128)}, f32[2,6,512,51...) while((s32[]{:T(128)}, ...), condition=%wide.region_27.28_spmd, body=%wide.region_25.27_spmd.sunk | while | flops 1227224064 | bytes 90919112 | solution.py:276
  544.3 4.2 bitcast_dynamic-update-slice_fusion.8
  562.1 4.2 bitcast_dynamic-update-slice_fusion.8
  583.3 5.4 bitcast_convert_fusion.1
  589.0 7.9 convolution_bitcast_fusion
  599.9 4.4 convolution_bitcast_fusion.4
  604.3 6.2 all-reduce.22.cloned.1.call-done
  610.5 4.9 multiply_reduce_fusion.4
  617.9 9.6 fusion.212
  633.0 5.6 convolution_bitcast_fusion.1
  638.7 7.4 pad_maximum_fusion.1
  646.2 4.9 convolution_bitcast_fusion.3
  654.7 4.2 multiply_reduce_fusion.5
  667.3 54.3 %while.57 = (s32[]{:T(128)}, bf16[2,512,6,64]{1,3,2,0:T(8,128)(2,1)}, bf16[2,512,6,64]{1,3,2,0:T(8,128)(2,1)}, f32[2,512,6,64]{1,3,2,0:T(8,128)}, bf16[2,512,6,6...) while((s32[]{:T(128)}, ...), condition=%wide.region_36.37_spmd, body=%wide.region_34.36_spmd.sunk | while | flops 1222512128 | bytes 87736576 | solution.py:276
  667.4 5.2 exponential_select_fusion.3
  672.6 7.6 fusion.310
  680.2 7.8 fusion.311
  694.4 5.2 exponential_select_fusion.3
  699.7 7.6 fusion.310
  707.3 7.8 fusion.311
  730.3 5.2 bitcast_convert_fusion
  735.8 8.5 pad_maximum_fusion
  757.3 4.5 add_reduce_fusion
  762.6 736.8 %all-reduce.30.cloned.1.call-done = (f32[2,768,3,384]{3,1,2,0:T(8,128)}, f32[2,768,384]{2,1,0:T(8,128)}, f32[2,768,1536]{2,1,0:T(8,128)}, f32[2,768,1536]{2,1,0:T(8,128)}) async-done(((f32[2,768,3,384]{3,1,2,0:T(8,128)}, f32[2,768,384]{2,1,0:T(8,128)}, f32[2,768,1536]{2,1,0:T(8,128)}, f32[2,768,1536]{2,1,0:T(8,128)}), (f32[2,768,3,384]{3,1,2,0:T(8,128)}, f32[2,768,384]{2,1,0:T(8,128)}, ...) | async-done | bytes 28311568 | tf_op jit(solution)/shard_map/psum | solution.py:323
  1509.1 114.0 %all-reduce.28.cloned.1.call-done = f32[2,8448]{1,0:T(2,128)} async-done(((f32[2,8448]{1,0:T(2,128)}), f32[2,8448]{1,0:T(2,128)}) %all-reduce.28.cloned.1.call-update) | async-done | bytes 67600 | tf_op jit(solution)/shard_map/psum | solution.py:337
  1624.7 42.6 %psum.117 = f32[]{:T(128)} all-reduce(f32[]{:T(128)S(6)} %add.422), channel_id=1, replica_groups=mesh['dp'=16,'tensor'=2] {'dp','tensor'}, use_global_device_ids=true, to_apply=%region_46.47 | all-reduce | flops 1 | bytes 8 | tf_op jit(solution)/shard_map/psum | solution.py:337
  1678.7 39.2 %psum.119 = f32[4,2]{0,1:T(2,128)S(1)} all-reduce(f32[4,2]{0,1:T(2,128)S(1)} %pad_maximum_fusion.12), channel_id=1, replica_groups=mesh['dp'=16,'tensor'=2] {'dp','tensor'}, use_global_device_ids=true, to_apply=%region_69.70 | all-reduce | flops 8 | bytes 64 | tf_op jit(solution)/shard_map/psum | solution.py:337
  1718.0 41.2 %all-gather.1 = f32[32,4,2]{1,2,0:T(2,128)S(1)} all-gather(f32[1,4,2]{1,2,0:T(2,128)S(1)} %bitcast.401), channel_id=2, replica_groups=mesh['dp'=16,'tensor'=2] {'dp','tensor'}, dimensions={0}, use_global_device_ids=true | all-gather | bytes 1056 | tf_op jit(solution)/shard_map/all_gather | solution.py:353
  (525 shorter events, 231.9 us)
Async XLA Ops:
  7.2 78.1 %all-gather.7.cloned.1.call-start = ((), (), s32[]{:S(2)}) async-start(), calls=%async_computation | async-start | bytes 3760128 | tf_op jit(solution)/shard_map/all_gather | solution.py:137
  9.0 134.3 %all-gather.9.cloned.1.call-start = ((), (), s32[]{:S(2)}) async-start(), calls=%async_computation.1 | async-start | bytes 1253376 | tf_op jit(solution)/shard_map/all_gather | solution.py:138
  10.6 155.7 %all-reduce.12.cloned.1.call-start = ((), (), s32[]{:S(2)}) async-start(), calls=%async_computation.2 | async-start | bytes 3145728 | tf_op jit(solution)/shard_map/psum | solution.py:181
  12.3 347.5 %copy-start.63 = (f32[768]{0:T(1024)}, f32[768]{0:T(1024)S(1)}, u32[]{:S(2)}) copy-start(f32[768]{0:T(1024)S(1)} %get-tuple-element.549) | copy-start | bytes 9220
  12.3 347.5 %copy-start.73 = (f32[768]{0:T(1024)}, f32[768]{0:T(1024)S(1)}, u32[]{:S(2)}) copy-start(f32[768]{0:T(1024)S(1)} %get-tuple-element.548) | copy-start | bytes 9220
  12.3 409.6 %copy-start.77 = (f32[768]{0:T(1024)}, f32[768]{0:T(1024)S(1)}, u32[]{:S(2)}) copy-start(f32[768]{0:T(1024)S(1)} %get-tuple-element.545) | copy-start | bytes 9220
  111.5 31.8 %copy-start.19 = (bf16[2,512,6,64]{1,3,2,0:T(8,128)(2,1)}, bf16[2,512,6,64]{1,3,2,0:T(8,128)(2,1)S(1)}, u32[]{:S(2)}) copy-start(bf16[2,512,6,64]{1,3,2,0:T(8,128)(2,1)S(1)} %get-tuple-element.1128) | copy-start | bytes 2359300
  112.4 34.6 %copy-start.33 = (f32[2,48,1536]{2,1,0:T(8,128)S(1)}, f32[2,48,1536]{2,1,0:T(8,128)}, u32[]{:S(2)}) copy-start(f32[2,48,1536]{2,1,0:T(8,128)} %param.31) | copy-start | bytes 1769476
  113.4 34.4 %copy-start.31 = (f32[2,48,1536]{2,1,0:T(8,128)S(1)}, f32[2,48,1536]{2,1,0:T(8,128)}, u32[]{:S(2)}) copy-start(f32[2,48,1536]{2,1,0:T(8,128)} %param.32) | copy-start | bytes 1769476
  143.3 23.1 %copy-start.10 = (bf16[1024,768]{1,0:T(8,128)(2,1)S(1)}, bf16[1024,768]{1,0:T(8,128)(2,1)}, u32[]{:S(2)}) copy-start(bf16[1024,768]{1,0:T(8,128)(2,1)} %param.26) | copy-start | bytes 4718596
  146.9 104.6 %all-gather.11.cloned.1.call-start = ((), (), s32[]{:S(2)}) async-start(), calls=%async_computation.3 | async-start | bytes 5013504 | tf_op jit(solution)/shard_map/all_gather | solution.py:139
  147.7 186.4 %all-gather.13.cloned.1.call-start = ((), (), s32[]{:S(2)}) async-start(), calls=%async_computation.4 | async-start | bytes 5013504 | tf_op jit(solution)/shard_map/all_gather | solution.py:140
  148.5 211.2 %all-reduce.14.cloned.1.call-start = ((), (), s32[]{:S(2)}) async-start(), calls=%async_computation.5 | async-start | bytes 3145728 | tf_op jit(solution)/shard_map/psum | solution.py:194
  149.7 101.8 %copy-start.105 = (f32[1536]{0:T(1024)}, f32[1536]{0:T(1024)S(1)}, u32[]{:S(2)}) copy-start(f32[1536]{0:T(1024)S(1)} %dynamic-slice_reduce_fusion.5) | copy-start | bytes 18436
  166.3 85.2 %copy-start.88 = (f32[768]{0:T(1024)S(1)}, f32[768]{0:T(1024)}, u32[]{:S(2)}) copy-start(f32[768]{0:T(1024)} %get-tuple-element.547) | copy-start | bytes 9220
  168.5 191.3 %copy-start.67 = (f32[1024]{0:T(1024)}, f32[1024]{0:T(1024)S(1)}, u32[]{:S(2)}) copy-start(f32[1024]{0:T(1024)S(1)} %broadcast_multiply_fusion.3) | copy-start | bytes 12292
  169.4 102.8 %copy-start.83 = (f32[1024]{0:T(1024)}, f32[1024]{0:T(1024)S(1)}, u32[]{:S(2)}) copy-start(f32[1024]{0:T(1024)S(1)} %multiply_reduce_fusion.13) | copy-start | bytes 12292
  169.4 190.3 %copy-start.75 = (f32[1024]{0:T(1024)}, f32[1024]{0:T(1024)S(1)}, u32[]{:S(2)}) copy-start(f32[1024]{0:T(1024)S(1)} %fusion.167) | copy-start | bytes 12292
  334.1 25.6 %copy-start.95 = (f32[768]{0:T(1024)S(1)}, f32[768]{0:T(1024)}, u32[]{:S(2)}) copy-start(f32[768]{0:T(1024)} %get-tuple-element.546) | copy-start | bytes 9220
  340.5 81.3 %all-reduce.16.cloned.1.call-start = ((), (), s32[]{:S(2)}) async-start(), calls=%async_computation.6 | async-start | bytes 3145728 | tf_op jit(solution)/shard_map/psum | solution.py:181
  363.1 58.8 %copy-start.69 = (f32[1024]{0:T(1024)}, f32[1024]{0:T(1024)S(1)}, u32[]{:S(2)}) copy-start(f32[1024]{0:T(1024)S(1)} %broadcast_multiply_fusion.2) | copy-start | bytes 12292
  363.6 58.3 %copy-start.80 = (f32[1024]{0:T(1024)}, f32[1024]{0:T(1024)S(1)}, u32[]{:S(2)}) copy-start(f32[1024]{0:T(1024)S(1)} %fusion.168) | copy-start | bytes 12292
  396.9 25.0 %copy-start.94 = (f32[768]{0:T(1024)S(1)}, f32[768]{0:T(1024)}, u32[]{:S(2)}) copy-start(f32[768]{0:T(1024)} %get-tuple-element.543) | copy-start | bytes 9220
  400.1 73.7 %all-reduce.18.cloned.1.call-start = ((), (), s32[]{:S(2)}) async-start(), calls=%async_computation.7 | async-start | bytes 3145728 | tf_op jit(solution)/shard_map/psum | solution.py:194
  425.5 19.5 %copy-start.3 = (f32[1024,768]{1,0:T(8,128)}, f32[1024,768]{1,0:T(8,128)S(1)}, u32[]{:S(2)}) copy-start(f32[1024,768]{1,0:T(8,128)S(1)} %get-tuple-element.663) | copy-start | bytes 9437188
  446.7 27.1 %copy-start.93 = (f32[768]{0:T(1024)S(1)}, f32[768]{0:T(1024)}, u32[]{:S(2)}) copy-start(f32[768]{0:T(1024)} %get-tuple-element.540) | copy-start | bytes 9220
  452.1 68.9 %all-reduce.20.cloned.1.call-start = ((), (), s32[]{:S(2)}) async-start(), calls=%async_computation.8 | async-start | bytes 3145728 | tf_op jit(solution)/shard_map/psum | solution.py:246
  481.3 14.2 slice-start.4
  484.3 11.2 slice-start.5
  499.2 111.2 %all-reduce.22.cloned.1.call-start = ((), (), s32[]{:S(2)}) async-start(), calls=%async_computation.9 | async-start | bytes 3145728 | tf_op jit(solution)/shard_map/psum | solution.py:293
  588.8 65.9 %all-reduce.24.cloned.1.call-start = ((), (), s32[]{:S(2)}) async-start(), calls=%async_computation.10 | async-start | bytes 3145728 | tf_op jit(solution)/shard_map/psum | solution.py:246
  616.1 13.1 slice-start.6
  617.9 11.3 slice-start.7
  632.9 124.3 %all-reduce.26.cloned.1.call-start = ((), (), s32[]{:S(2)}) async-start(), calls=%async_computation.11 | async-start | bytes 3145728 | tf_op jit(solution)/shard_map/psum | solution.py:293
  672.6 19.9 %slice-start = ((s8[6291456]{0:T(1024)(128)(4,1)}), s8[2097152]{0:T(1024)(128)(4,1)S(1)}, s32[]{:S(2)}) async-start(s8[6291456]{0:T(1024)(128)(4,1)} %bitcast.393), calls=%async_computation.14 | async-start | bytes 4194304 | tf_op jit(solution)/shard_map/while
  680.2 12.3 slice-start.1
  699.7 19.9 %slice-start = ((s8[6291456]{0:T(1024)(128)(4,1)}), s8[2097152]{0:T(1024)(128)(4,1)S(1)}, s32[]{:S(2)}) async-start(s8[6291456]{0:T(1024)(128)(4,1)} %bitcast.393), calls=%async_computation.14 | async-start | bytes 4194304 | tf_op jit(solution)/shard_map/while
  707.2 12.3 slice-start.1
  735.6 763.9 %all-reduce.30.cloned.1.call-start = ((), (), s32[]{:S(2)}) async-start(), calls=%async_computation.13 | async-start | bytes 56623104 | tf_op jit(solution)/shard_map/psum | solution.py:323
  753.9 869.2 %all-reduce.28.cloned.1.call-start = ((), (), s32[]{:S(2)}) async-start(), calls=%async_computation.12 | async-start | bytes 135168 | tf_op jit(solution)/shard_map/psum | solution.py:337
  755.8 912.9 %copy-start.46 = (f32[2,48,384]{2,1,0:T(8,128)S(1)}, f32[2,48,384]{2,1,0:T(8,128)}, u32[]{:S(2)}) copy-start(f32[2,48,384]{2,1,0:T(8,128)} %param.30) | copy-start | bytes 442372
  755.8 912.9 %copy-start.65 = (f32[2,48,384]{2,1,0:T(8,128)S(1)}, f32[2,48,384]{2,1,0:T(8,128)}, u32[]{:S(2)}) copy-start(f32[2,48,384]{2,1,0:T(8,128)} %param.36) | copy-start | bytes 442372
  755.8 912.9 %copy-start.66 = (f32[2,48,384]{2,1,0:T(8,128)S(1)}, f32[2,48,384]{2,1,0:T(8,128)}, u32[]{:S(2)}) copy-start(f32[2,48,384]{2,1,0:T(8,128)} %param.37) | copy-start | bytes 442372
  761.8 908.7 %copy-start.34 = (f32[2,48,1536]{2,1,0:T(8,128)S(1)}, f32[2,48,1536]{2,1,0:T(8,128)}, u32[]{:S(2)}) copy-start(f32[2,48,1536]{2,1,0:T(8,128)} %param.31) | copy-start | bytes 1769476
  1499.5 173.2 %copy-start.32 = (f32[2,48,1536]{2,1,0:T(8,128)S(1)}, f32[2,48,1536]{2,1,0:T(8,128)}, u32[]{:S(2)}) copy-start(f32[2,48,1536]{2,1,0:T(8,128)} %param.32) | copy-start | bytes 1769476
  1672.6 89.3 %copy-start.42 = (f32[2,48,1536]{2,1,0:T(8,128)}, f32[2,48,1536]{2,1,0:T(8,128)S(1)}, u32[]{:S(2)}) copy-start(f32[2,48,1536]{2,1,0:T(8,128)S(1)} %get-tuple-element.646) | copy-start | bytes 1769476
  1672.6 89.3 %copy-start.43 = (f32[2,48,1536]{2,1,0:T(8,128)}, f32[2,48,1536]{2,1,0:T(8,128)S(1)}, u32[]{:S(2)}) copy-start(f32[2,48,1536]{2,1,0:T(8,128)S(1)} %get-tuple-element.647) | copy-start | bytes 1769476
  1678.5 87.3 %copy-start.44 = (f32[2,48,3,384]{3,1,2,0:T(8,128)}, f32[2,48,3,384]{3,1,2,0:T(8,128)S(1)}, u32[]{:S(2)}) copy-start(f32[2,48,3,384]{3,1,2,0:T(8,128)S(1)} %get-tuple-element.642) | copy-start | bytes 1327108
  (99 other events, 403.3 us)
Sparse Core Ops, SparseCore 0:
  11.3 73.9 all-gather.6
  88.5 54.6 all-gather.8
  147.0 19.2 all-reduce.11
  169.8 81.6 all-gather.10
  255.0 79.0 all-gather.12
  340.7 19.0 all-reduce.13
  400.2 21.5 all-reduce.15
  452.2 21.5 all-reduce.17
  499.4 21.5 all-reduce.19
  588.9 21.5 all-reduce.21
  633.1 21.5 all-reduce.23
  735.7 21.5 all-reduce.25
  763.7 735.7 all-reduce.29
  1506.4 116.6 all-reduce.27
